TPU v7x, 256 devices: a whole 4x4x8 slice. The times are simulated.
256 devices in a mesh: site: 2 (over core), wide: 32 (over x, z), narrow: 4 (over y).
Axes of the slice: x: 4, y: 4, z: 8, core: 2. Of those that a mesh axis runs over, the one named last changes fastest.
Arguments:
- initial_rows: float32 [64, 4, 2048], P('site', 'narrow'), may hold values from -6 to 6
- outcomes: int32 [64, 4], replicated, may hold values 0 or 1
- tensors: float32 [4, 2, 4, 2048, 8192], P('site', None, 'narrow', None, 'wide'), may hold values from -0.25 to 0.25
Outputs:
- final_rows: float32 [64, 4, 2048], P('site', 'narrow')
- log_weight: float32 [64], P('site')
All inputs are finite; a program needn't handle non-finite values.
Results may differ from a plain program's by a relative error of at most 0.0003.
Values sent between devices are 32-bit elements; how exact they have to be, the bound alone decides.
A program may use at most 64 MiB of HBM per device.

v0:
```python
import jax
import jax.numpy as jnp
from jax import lax
from jax.sharding import PartitionSpec as P

BOND = 8192
epsilon = 1e-06
highest = lax.Precision.HIGHEST


def from_partner(value, axis, distance):
    mask = 2**distance
    pairs = [(source, source ^ mask) for source in range(lax.axis_size(axis))]
    return lax.ppermute(value, axis, pairs)


def advance(held, log_sum, site_tensor, chosen):
    front = held.shape[0]
    groups = lax.axis_size("narrow")
    share = front // groups
    summed = lax.psum_scatter(
        jnp.einsum(
            "bar,oard->bod",
            held,
            site_tensor,
            precision=highest,
            preferred_element_type=jnp.float32,
        ),
        "narrow",
        scatter_dimension=0,
        tiled=True,
    )
    local_choice = lax.dynamic_slice_in_dim(chosen, lax.axis_index("narrow") * share, share, 0)
    squares = jnp.sum(summed * summed, axis=2)
    raw_kept = jnp.where(local_choice[:, None] == 0, summed[:, 0, :], summed[:, 1, :])
    totals = lax.psum(squares, "wide")
    both_mean = (totals[:, 0] + totals[:, 1]) / (2.0 * BOND)
    scale = lax.rsqrt(both_mean + epsilon)
    full_rows = lax.all_gather(raw_kept * scale[:, None], "wide", axis=1, tiled=True)
    kept_square = jnp.where(local_choice == 0, totals[:, 0], totals[:, 1])
    local_ratio = jnp.log(kept_square / BOND + epsilon) - jnp.log(both_mean + epsilon)
    ratio_table = jnp.broadcast_to(local_ratio[:, None], (share, groups))
    split_rows = full_rows.reshape(share, groups, -1)
    moved, moved_ratio = (
        lax.all_to_all(split_rows, "narrow", split_axis=1, concat_axis=0, tiled=True),
        lax.all_to_all(ratio_table, "narrow", split_axis=1, concat_axis=0, tiled=True),
    )
    return (moved, log_sum + moved_ratio[:, 0])


def run_section(held, log_sum, tensors, chosen_block):
    for local_site in range(tensors.shape[0]):
        held, log_sum = advance(held, log_sum, tensors[local_site], chosen_block[:, local_site])
    return (held, log_sum)


def hand_over(held, log_sum):
    moved_rows, moved_sum = from_partner((held, log_sum), "site", 0)
    return (moved_rows, moved_sum)


def shards(initial_rows, outcomes, tensors):
    section = lax.axis_index("site")
    front = initial_rows.shape[0]
    local_count = tensors.shape[0]
    section_columns = lax.dynamic_slice_in_dim(outcomes, section * local_count, local_count, 1)
    held = initial_rows
    log_sum = jnp.zeros((front,), jnp.float32)
    front_order = (section, 1 - section, section)
    for turn_index in range(3):
        new_rows, new_sum = run_section(
            held,
            log_sum,
            tensors,
            lax.dynamic_slice_in_dim(section_columns, front_order[turn_index] * front, front, 0),
        )
        if turn_index == 1:
            held, log_sum = (new_rows, new_sum)
        else:
            active = section == 0 if turn_index == 0 else section == 1
            held = jnp.where(active, new_rows, held)
            log_sum = jnp.where(active, new_sum, log_sum)
        if turn_index < 2:
            held, log_sum = hand_over(held, log_sum)
    return (held, log_sum)


def solution(mesh):
    placed = (P("site", "narrow", None), P(), P("site", None, "narrow", None, "wide"))
    return jax.shard_map(
        shards,
        mesh=mesh,
        in_specs=placed,
        out_specs=(P("site", "narrow", None), P("site")),
        check_vma=False,
    )
```

profile of v0, /device:TPU:2, one launch (start us, length us, event | category | flops | bytes accessed | tf_op | source)
XLA Modules:
  0.0 993.4 jit_solution(1777501969221541964)
XLA Ops:
  7.2 5.4 fusion.2
  13.6 25.4 %reduce-scatter.7.cloned.1.call-done = f32[8,2,256]{2,0,1:T(8,128)} async-done(((f32[32,2,256]{2,0,1:T(8,128)}), f32[8,2,256]{2,0,1:T(8,128)}) %reduce-scatter.7.cloned.1.call-update) | async-done | bytes 16400 | tf_op jit(solution)/shard_map/reduce_scatter | solution.py:21
  39.8 63.2 %psum.42 = f32[8,2]{0,1:T(2,128)S(1)} all-reduce(f32[8,2]{0,1:T(2,128)S(1)} %multiply_reduce_fusion.5), channel_id=1, replica_groups=mesh['site'=2,'wide'=32,'narrow'=4] {'wide'}, use_global_device_ids=true, to_apply=%region_2.3 | all-reduce | flops 16 | bytes 128 | tf_op jit(solution)/shard_map/psum | solution.py:36
  103.9 58.4 %all_gather.18 = f32[8,8192]{1,0:T(8,128)S(1)} all-gather(f32[8,256]{1,0:T(8,128)S(1)} %fusion.24), channel_id=1, replica_groups=mesh['site'=2,'wide'=32,'narrow'=4] {'wide'}, dimensions={1}, use_global_device_ids=true | all-gather | bytes 270336 | tf_op jit(solution)/shard_map/all_gather | solution.py:39
  162.3 9.2 all_to_all.171
  171.5 5.3 fusion.5
  176.9 18.2 %reduce-scatter.9.cloned.1.call-done = f32[8,2,256]{2,0,1:T(8,128)} async-done(((f32[32,2,256]{2,0,1:T(8,128)}), f32[8,2,256]{2,0,1:T(8,128)}) %reduce-scatter.9.cloned.1.call-update) | async-done | bytes 16400 | tf_op jit(solution)/shard_map/reduce_scatter | solution.py:21
  195.9 63.2 %psum.43 = f32[8,2]{0,1:T(2,128)S(1)} all-reduce(f32[8,2]{0,1:T(2,128)S(1)} %multiply_reduce_fusion.4), channel_id=1, replica_groups=mesh['site'=2,'wide'=32,'narrow'=4] {'wide'}, use_global_device_ids=true, to_apply=%region_5.6 | all-reduce | flops 16 | bytes 128 | tf_op jit(solution)/shard_map/psum | solution.py:36
  260.0 62.4 %all_gather.19 = f32[8,8192]{1,0:T(8,128)} all-gather(f32[8,256]{1,0:T(8,128)S(1)} %fusion.22), channel_id=1, replica_groups=mesh['site'=2,'wide'=32,'narrow'=4] {'wide'}, dimensions={1}, use_global_device_ids=true | all-gather | bytes 270336 | tf_op jit(solution)/shard_map/all_gather | solution.py:39
  325.9 6.6 all-to-all-done.1
  334.2 5.3 fusion.1
  339.6 18.2 %reduce-scatter.11.cloned.1.call-done = f32[8,2,256]{2,0,1:T(8,128)} async-done(((f32[32,2,256]{2,0,1:T(8,128)}), f32[8,2,256]{2,0,1:T(8,128)}) %reduce-scatter.11.cloned.1.call-update) | async-done | bytes 16400 | tf_op jit(solution)/shard_map/reduce_scatter | solution.py:21
  358.6 63.2 %psum.44 = f32[8,2]{0,1:T(2,128)S(1)} all-reduce(f32[8,2]{0,1:T(2,128)S(1)} %multiply_reduce_fusion.3), channel_id=1, replica_groups=mesh['site'=2,'wide'=32,'narrow'=4] {'wide'}, use_global_device_ids=true, to_apply=%region_8.9 | all-reduce | flops 16 | bytes 128 | tf_op jit(solution)/shard_map/psum | solution.py:36
  422.8 58.4 %all_gather.20 = f32[8,8192]{1,0:T(8,128)S(1)} all-gather(f32[8,256]{1,0:T(8,128)S(1)} %fusion.20), channel_id=1, replica_groups=mesh['site'=2,'wide'=32,'narrow'=4] {'wide'}, dimensions={1}, use_global_device_ids=true | all-gather | bytes 270336 | tf_op jit(solution)/shard_map/all_gather | solution.py:39
  481.1 9.2 all_to_all.172
  490.3 5.3 fusion.4
  495.7 18.1 %reduce-scatter.13.cloned.1.call-done = f32[8,2,256]{2,0,1:T(8,128)} async-done(((f32[32,2,256]{2,0,1:T(8,128)}), f32[8,2,256]{2,0,1:T(8,128)}) %reduce-scatter.13.cloned.1.call-update) | async-done | bytes 16400 | tf_op jit(solution)/shard_map/reduce_scatter | solution.py:21
  514.7 63.2 %psum.45 = f32[8,2]{0,1:T(2,128)S(1)} all-reduce(f32[8,2]{0,1:T(2,128)S(1)} %multiply_reduce_fusion.2), channel_id=1, replica_groups=mesh['site'=2,'wide'=32,'narrow'=4] {'wide'}, use_global_device_ids=true, to_apply=%region_11.12 | all-reduce | flops 16 | bytes 128 | tf_op jit(solution)/shard_map/psum | solution.py:36
  578.8 58.4 %all_gather.21 = f32[8,8192]{1,0:T(8,128)S(1)} all-gather(f32[8,256]{1,0:T(8,128)S(1)} %fusion.18), channel_id=1, replica_groups=mesh['site'=2,'wide'=32,'narrow'=4] {'wide'}, dimensions={1}, use_global_device_ids=true | all-gather | bytes 270336 | tf_op jit(solution)/shard_map/all_gather | solution.py:39
  637.2 9.2 all_to_all.173
  647.9 5.3 fusion
  653.3 7.6 all_to_all.174
  664.6 5.2 all-to-all-done.7
  676.0 63.3 %psum.46 = f32[8,2]{0,1:T(2,128)S(1)} all-reduce(f32[8,2]{0,1:T(2,128)S(1)} %multiply_reduce_fusion.1), channel_id=1, replica_groups=mesh['site'=2,'wide'=32,'narrow'=4] {'wide'}, use_global_device_ids=true, to_apply=%region_14.15 | all-reduce | flops 16 | bytes 128 | tf_op jit(solution)/shard_map/psum | solution.py:36
  745.5 62.4 %all_gather.22 = f32[8,8192]{1,0:T(8,128)} all-gather(f32[8,256]{1,0:T(8,128)S(1)} %fusion.16), channel_id=1, replica_groups=mesh['site'=2,'wide'=32,'narrow'=4] {'wide'}, dimensions={1}, use_global_device_ids=true | all-gather | bytes 270336 | tf_op jit(solution)/shard_map/all_gather | solution.py:39
  812.9 6.5 all-to-all-done.4
  819.4 5.3 fusion.3
  828.6 5.1 all-to-all-done.10
  833.7 9.2 reduce-scatter.17.cloned.1.call-done
  843.8 63.2 %psum.47 = f32[8,2]{0,1:T(2,128)S(1)} all-reduce(f32[8,2]{0,1:T(2,128)S(1)} %multiply_reduce_fusion), channel_id=1, replica_groups=mesh['site'=2,'wide'=32,'narrow'=4] {'wide'}, use_global_device_ids=true, to_apply=%region_17.18 | all-reduce | flops 16 | bytes 128 | tf_op jit(solution)/shard_map/psum | solution.py:36
  911.7 62.4 %all_gather.23 = f32[8,8192]{1,0:T(8,128)} all-gather(f32[8,256]{1,0:T(8,128)S(1)} %fusion.14), channel_id=1, replica_groups=mesh['site'=2,'wide'=32,'narrow'=4] {'wide'}, dimensions={1}, use_global_device_ids=true | all-gather | bytes 270336 | tf_op jit(solution)/shard_map/all_gather | solution.py:39
  979.5 6.1 all-to-all-done.5
  (80 shorter events, 51.7 us)
Async XLA Ops:
  7.2 325.3 %copy-start = (f32[32,1,2048]{2,1,0:T(1,128)S(1)}, f32[32,1,2048]{2,1,0:T(1,128)}, u32[]{:S(2)}) copy-start(f32[32,1,2048]{2,1,0:T(1,128)} %param.3) | copy-start | bytes 786436
  7.2 31.8 %reduce-scatter.7.cloned.1.call-start = ((), (), s32[]{:S(2)}) async-start(), calls=%async_computation.18 | async-start | bytes 81920 | tf_op jit(solution)/shard_map/reduce_scatter | solution.py:21
  12.7 182.3 %reduce-scatter.9.cloned.1.call-start = ((), (), s32[]{:S(2)}) async-start(), calls=%async_computation.19 | async-start | bytes 81920 | tf_op jit(solution)/shard_map/reduce_scatter | solution.py:21
  322.4 10.1 %all-to-all-start.1 = ((f32[8,4,2048]{2,0,1:T(8,128)}), f32[8,4,2048]{2,0,1:T(8,128)S(1)}, u32[]{:S(2)}, u32[]{:S(2)}) async-start(f32[8,4,2048]{2,0,1:T(8,128)} %bitcast.19), calls=%async_computation.3 | async-start | bytes 524288 | tf_op jit(solution)/shard_map/all_to_all | solution.py:45
  325.8 31.9 %reduce-scatter.11.cloned.1.call-start = ((), (), s32[]{:S(2)}) async-start(), calls=%async_computation.20 | async-start | bytes 81920 | tf_op jit(solution)/shard_map/reduce_scatter | solution.py:21
  332.6 1.6 collective-permute-start
  339.5 174.3 %reduce-scatter.13.cloned.1.call-start = ((), (), s32[]{:S(2)}) async-start(), calls=%async_computation.21 | async-start | bytes 81920 | tf_op jit(solution)/shard_map/reduce_scatter | solution.py:21
  495.6 175.8 %reduce-scatter.15.cloned.1.call-start = ((), (), s32[]{:S(2)}) async-start(), calls=%async_computation.22 | async-start | bytes 81920 | tf_op jit(solution)/shard_map/reduce_scatter | solution.py:21
  646.4 1.5 collective-permute-start.1
  661.5 8.4 all-to-all-start.7
  670.0 154.7 %collective-permute-start.2 = (f32[32]{0:T(128)S(1)}, f32[32]{0:T(128)S(1)}, u32[]{:S(2)}, u32[]{:S(2)}) collective-permute-start(f32[32]{0:T(128)S(1)} %select_n.125), channel_id=1, source_target_pairs={{0,128},{128,0},{1,129},{129,1},{2,130},{130,2},{3,131},{131,3},{4... | collective-permute-start | bytes 392 | tf_op jit(solution)/shard_map/ppermute | solution.py:14
  672.8 67.4 %all-to-all-start.8 = ((f32[8,4,1]{0,2,1:T(1,128)}), f32[8,4,1]{0,2,1:T(1,128)S(1)}, u32[]{:S(2)}, u32[]{:S(2)}) async-start(f32[8,4,1]{0,2,1:T(1,128)} %broadcast_in_dim.99), calls=%async_computation.14 | async-start | bytes 4096 | tf_op jit(solution)/shard_map/all_to_all | solution.py:46
  740.7 67.1 %all-to-all-start.9 = ((f32[8,4,1]{0,2,1:T(1,128)}), f32[8,4,1]{0,2,1:T(1,128)S(1)}, u32[]{:S(2)}, u32[]{:S(2)}) async-start(f32[8,4,1]{0,2,1:T(1,128)} %broadcast_in_dim.100), calls=%async_computation.15 | async-start | bytes 4096 | tf_op jit(solution)/shard_map/all_to_all | solution.py:46
  807.9 11.5 %all-to-all-start.4 = ((f32[8,4,2048]{2,0,1:T(8,128)}), f32[8,4,2048]{2,0,1:T(8,128)S(1)}, u32[]{:S(2)}, u32[]{:S(2)}) async-start(f32[8,4,2048]{2,0,1:T(8,128)} %bitcast.45), calls=%async_computation.9 | async-start | bytes 524288 | tf_op jit(solution)/shard_map/all_to_all | solution.py:45
  812.7 30.3 %reduce-scatter.17.cloned.1.call-start = ((), (), s32[]{:S(2)}) async-start(), calls=%async_computation.23 | async-start | bytes 81920 | tf_op jit(solution)/shard_map/reduce_scatter | solution.py:21
  825.3 8.4 all-to-all-start.10
  828.5 150.6 %collective-permute-start.3 = (f32[32]{0:T(128)S(1)}, f32[32]{0:T(128)S(1)}, u32[]{:S(2)}, u32[]{:S(2)}) collective-permute-start(f32[32]{0:T(128)S(1)} %add_add_fusion), channel_id=1, source_target_pairs={{0,128},{128,0},{1,129},{129,1},{2,130},{130,2},{3,131},{131,3},{4... | collective-permute-start | bytes 392 | tf_op jit(solution)/shard_map/ppermute | solution.py:14
  907.7 66.4 %all-to-all-start.11 = ((f32[8,4,1]{0,2,1:T(1,128)}), f32[8,4,1]{0,2,1:T(1,128)S(1)}, u32[]{:S(2)}, u32[]{:S(2)}) async-start(f32[8,4,1]{0,2,1:T(1,128)} %broadcast_in_dim.102), calls=%async_computation.17 | async-start | bytes 4096 | tf_op jit(solution)/shard_map/all_to_all | solution.py:46
  974.1 11.4 %all-to-all-start.5 = ((f32[8,4,2048]{2,0,1:T(8,128)}), f32[8,4,2048]{2,0,1:T(8,128)S(1)}, u32[]{:S(2)}, u32[]{:S(2)}) async-start(f32[8,4,2048]{2,0,1:T(8,128)} %bitcast.53), calls=%async_computation.11 | async-start | bytes 524288 | tf_op jit(solution)/shard_map/all_to_all | solution.py:45
Sparse Core Ops, SparseCore 0:
  12.8 26.1 reduce-scatter.6
  177.0 18.0 reduce-scatter.8
  339.6 18.0 reduce-scatter.10
  495.8 18.0 reduce-scatter.12
  653.4 18.0 reduce-scatter.14
  824.8 18.0 reduce-scatter.16
where the time goes:
time: 995 us; the launch traced here: 993 us
  blocking collectives  777 us (78%)
  waiting for transfers between devices  123 us (12%)
  matrix products  31.9 us (3%)
  starting transfers between devices  30.9 us (3%)
  between operations  14.3 us (1%)
  other arithmetic  11 us (1%)
    psum x6, blocking collectives, advance(): totals = lax.psum(squares, 'wide')  379 us
    all_gather x6, blocking collectives, advance(): lax.all_gather(raw_kept * scale[:, None], 'wide', axis=1, tiled=True)  362 us
    reduce_scatter x6, waiting for transfers between devices, advance(): lax.psum_scatter(jnp.einsum('bar,oard->bod', held, site_tensor, precision...  90.4 us
    dot_general x6, matrix products, advance(): jnp.einsum('bar,oard->bod', held, site_tensor, precision=highest, preferr...  31.9 us
    all_to_all x3, blocking collectives, advance(): lax.all_to_all(split_rows, 'narrow', split_axis=1, concat_axis=0, tiled=T...  27.6 us
  transfers between devices with their start and end apart: 18, of which 13 were waited for; matrix products, arithmetic and copies ran while one was open for 1% of the time, Pallas kernels for 0%

commit v1 on v0

--- a/solution.py
+++ b/solution.py
@@ -33,7 +33,8 @@
     local_choice = lax.dynamic_slice_in_dim(chosen, lax.axis_index("narrow") * share, share, 0)
     squares = jnp.sum(summed * summed, axis=2)
     raw_kept = jnp.where(local_choice[:, None] == 0, summed[:, 0, :], summed[:, 1, :])
-    totals = lax.psum(squares, "wide")
+    terms = lax.all_gather(squares, "wide", axis=0, tiled=False)
+    totals = terms.sum(axis=0)
     both_mean = (totals[:, 0] + totals[:, 1]) / (2.0 * BOND)
     scale = lax.rsqrt(both_mean + epsilon)
     full_rows = lax.all_gather(raw_kept * scale[:, None], "wide", axis=1, tiled=True)

time: 995 us -> 817 us (0.82)
  blocking collectives: 777 us -> 589 us
  waiting for transfers between devices: 123 us -> 133 us
    psum x6 -> x0, blocking collectives: 379 us -> none  [advance(): totals = lax.psum(squares, 'wide')]
    all_gather x0 -> x6, blocking collectives: none -> 258 us  [advance(): terms = lax.all_gather(squares, 'wide', axis=0, tiled=False)]
    all_gather x6, blocking collectives: 362 us -> 296 us  [advance(): lax.all_gather(raw_kept * scale[:, None], 'wide', axis=1, tiled=True)]
    reduce_scatter x6, waiting for transfers between devices: 90.4 us -> 100 us  [advance(): lax.psum_scatter(jnp.einsum('bar,oard->bod', held, site_tensor, precision...]
  transfers between devices with their start and end apart: 18 -> 18, of which waited for: 13 -> 13; matrix products, arithmetic and copies ran while one was open for 1% -> 2% of each run, Pallas kernels for 0% -> 0%
where the time goes in v1:
time: 817 us; the launch traced here: 815 us
  blocking collectives  589 us (72%)
  waiting for transfers between devices  133 us (16%)
  matrix products  31.9 us (4%)
  starting transfers between devices  29.3 us (4%)
  between operations  14.3 us (2%)
  other arithmetic  11.3 us (1%)
    all_gather x6, blocking collectives, advance(): lax.all_gather(raw_kept * scale[:, None], 'wide', axis=1, tiled=True)  296 us
    all_gather x6, blocking collectives, advance(): terms = lax.all_gather(squares, 'wide', axis=0, tiled=False)  258 us
    reduce_scatter x6, waiting for transfers between devices, advance(): lax.psum_scatter(jnp.einsum('bar,oard->bod', held, site_tensor, precision...  100 us
    dot_general x6, matrix products, advance(): jnp.einsum('bar,oard->bod', held, site_tensor, precision=highest, preferr...  31.9 us
    all_to_all x3, blocking collectives, advance(): lax.all_to_all(split_rows, 'narrow', split_axis=1, concat_axis=0, tiled=T...  27.6 us
    all_to_all x3, waiting for transfers between devices, advance(): lax.all_to_all(split_rows, 'narrow', split_axis=1, concat_axis=0, tiled=T...  19.1 us
  transfers between devices with their start and end apart: 18, of which 13 were waited for; matrix products, arithmetic and copies ran while one was open for 2% of the time, Pallas kernels for 0%

profile of v1, /device:TPU:2, one launch (start us, length us, event | category | flops | bytes accessed | tf_op | source)
XLA Modules:
  0.0 814.7 jit_solution(17735559391198883577)
XLA Ops:
  7.2 5.4 fusion.2
  13.7 25.3 %reduce-scatter.7.cloned.1.call-done = f32[8,2,256]{2,0,1:T(8,128)} async-done(((f32[32,2,256]{2,0,1:T(8,128)}), f32[8,2,256]{2,0,1:T(8,128)}) %reduce-scatter.7.cloned.1.call-update) | async-done | bytes 16400 | tf_op jit(solution)/shard_map/reduce_scatter | solution.py:21
  39.8 43.0 %all-gather.6 = f32[32,8,2]{1,2,0:T(2,128)S(1)} all-gather(f32[1,8,2]{1,2,0:T(2,128)S(1)} %bitcast.193), channel_id=2, replica_groups=mesh['site'=2,'wide'=32,'narrow'=4] {'wide'}, dimensions={0}, use_global_device_ids=true | all-gather | bytes 2112 | tf_op jit(solution)/shard_map/all_gather | solution.py:36
  83.7 47.4 %all_gather.56 = f32[8,8192]{1,0:T(8,128)S(1)} all-gather(f32[8,256]{1,0:T(8,128)S(1)} %fusion.24), channel_id=1, replica_groups=mesh['site'=2,'wide'=32,'narrow'=4] {'wide'}, dimensions={1}, use_global_device_ids=true | all-gather | bytes 270336 | tf_op jit(solution)/shard_map/all_gather | solution.py:40
  131.1 9.2 %all_to_all.171 = f32[8,4,2048]{2,0,1:T(8,128)S(1)} all-to-all(f32[8,4,2048]{2,0,1:T(8,128)S(1)} %bitcast.189), channel_id=1, replica_groups=mesh['site'=2,'wide'=32,'narrow'=4] {'narrow'}, dimensions={1} | all-to-all | bytes 524288 | tf_op jit(solution)/shard_map/all_to_all | solution.py:46
  140.3 5.3 fusion.5
  145.7 20.9 %reduce-scatter.9.cloned.1.call-done = f32[8,2,256]{2,0,1:T(8,128)} async-done(((f32[32,2,256]{2,0,1:T(8,128)}), f32[8,2,256]{2,0,1:T(8,128)}) %reduce-scatter.9.cloned.1.call-update) | async-done | bytes 16400 | tf_op jit(solution)/shard_map/reduce_scatter | solution.py:21
  167.4 43.0 %all-gather.7 = f32[32,8,2]{1,2,0:T(2,128)S(1)} all-gather(f32[1,8,2]{1,2,0:T(2,128)S(1)} %bitcast.194), channel_id=3, replica_groups=mesh['site'=2,'wide'=32,'narrow'=4] {'wide'}, dimensions={0}, use_global_device_ids=true | all-gather | bytes 2112 | tf_op jit(solution)/shard_map/all_gather | solution.py:36
  211.3 51.4 %all_gather.59 = f32[8,8192]{1,0:T(8,128)} all-gather(f32[8,256]{1,0:T(8,128)S(1)} %fusion.22), channel_id=1, replica_groups=mesh['site'=2,'wide'=32,'narrow'=4] {'wide'}, dimensions={1}, use_global_device_ids=true | all-gather | bytes 270336 | tf_op jit(solution)/shard_map/all_gather | solution.py:40
  266.2 6.6 all-to-all-done.1
  274.5 5.3 fusion.1
  280.0 20.9 %reduce-scatter.11.cloned.1.call-done = f32[8,2,256]{2,0,1:T(8,128)} async-done(((f32[32,2,256]{2,0,1:T(8,128)}), f32[8,2,256]{2,0,1:T(8,128)}) %reduce-scatter.11.cloned.1.call-update) | async-done | bytes 16400 | tf_op jit(solution)/shard_map/reduce_scatter | solution.py:21
  301.7 43.0 %all-gather.8 = f32[32,8,2]{1,2,0:T(2,128)S(1)} all-gather(f32[1,8,2]{1,2,0:T(2,128)S(1)} %bitcast.195), channel_id=4, replica_groups=mesh['site'=2,'wide'=32,'narrow'=4] {'wide'}, dimensions={0}, use_global_device_ids=true | all-gather | bytes 2112 | tf_op jit(solution)/shard_map/all_gather | solution.py:36
  345.6 47.4 %all_gather.62 = f32[8,8192]{1,0:T(8,128)S(1)} all-gather(f32[8,256]{1,0:T(8,128)S(1)} %fusion.20), channel_id=1, replica_groups=mesh['site'=2,'wide'=32,'narrow'=4] {'wide'}, dimensions={1}, use_global_device_ids=true | all-gather | bytes 270336 | tf_op jit(solution)/shard_map/all_gather | solution.py:40
  393.0 9.2 %all_to_all.172 = f32[8,4,2048]{2,0,1:T(8,128)S(1)} all-to-all(f32[8,4,2048]{2,0,1:T(8,128)S(1)} %bitcast.190), channel_id=1, replica_groups=mesh['site'=2,'wide'=32,'narrow'=4] {'narrow'}, dimensions={1} | all-to-all | bytes 524288 | tf_op jit(solution)/shard_map/all_to_all | solution.py:46
  402.2 5.3 fusion.4
  407.6 20.9 %reduce-scatter.13.cloned.1.call-done = f32[8,2,256]{2,0,1:T(8,128)} async-done(((f32[32,2,256]{2,0,1:T(8,128)}), f32[8,2,256]{2,0,1:T(8,128)}) %reduce-scatter.13.cloned.1.call-update) | async-done | bytes 16400 | tf_op jit(solution)/shard_map/reduce_scatter | solution.py:21
  429.3 43.0 %all-gather.9 = f32[32,8,2]{1,2,0:T(2,128)S(1)} all-gather(f32[1,8,2]{1,2,0:T(2,128)S(1)} %bitcast.196), channel_id=5, replica_groups=mesh['site'=2,'wide'=32,'narrow'=4] {'wide'}, dimensions={0}, use_global_device_ids=true | all-gather | bytes 2112 | tf_op jit(solution)/shard_map/all_gather | solution.py:36
  473.2 47.4 %all_gather.65 = f32[8,8192]{1,0:T(8,128)S(1)} all-gather(f32[8,256]{1,0:T(8,128)S(1)} %fusion.18), channel_id=1, replica_groups=mesh['site'=2,'wide'=32,'narrow'=4] {'wide'}, dimensions={1}, use_global_device_ids=true | all-gather | bytes 270336 | tf_op jit(solution)/shard_map/all_gather | solution.py:40
  520.6 9.2 %all_to_all.173 = f32[8,4,2048]{2,0,1:T(8,128)S(1)} all-to-all(f32[8,4,2048]{2,0,1:T(8,128)S(1)} %bitcast.191), channel_id=1, replica_groups=mesh['site'=2,'wide'=32,'narrow'=4] {'narrow'}, dimensions={1} | all-to-all | bytes 524288 | tf_op jit(solution)/shard_map/all_to_all | solution.py:46
  531.4 5.3 fusion
  536.7 7.6 all_to_all.174
  548.1 5.3 all-to-all-done.7
  558.5 42.9 %all-gather.10 = f32[32,8,2]{1,2,0:T(2,128)S(1)} all-gather(f32[1,8,2]{1,2,0:T(2,128)S(1)} %bitcast.197), channel_id=6, replica_groups=mesh['site'=2,'wide'=32,'narrow'=4] {'wide'}, dimensions={0}, use_global_device_ids=true | all-gather | bytes 2112 | tf_op jit(solution)/shard_map/all_gather | solution.py:36
  606.2 51.4 %all_gather.68 = f32[8,8192]{1,0:T(8,128)} all-gather(f32[8,256]{1,0:T(8,128)S(1)} %fusion.16), channel_id=1, replica_groups=mesh['site'=2,'wide'=32,'narrow'=4] {'wide'}, dimensions={1}, use_global_device_ids=true | all-gather | bytes 270336 | tf_op jit(solution)/shard_map/all_gather | solution.py:40
  662.6 6.5 all-to-all-done.4
  669.0 5.3 fusion.3
  678.2 5.1 all-to-all-done.10
  683.5 11.9 %reduce-scatter.17.cloned.1.call-done = f32[8,2,256]{2,0,1:T(8,128)} async-done(((f32[32,2,256]{2,0,1:T(8,128)}), f32[8,2,256]{2,0,1:T(8,128)}) %reduce-scatter.17.cloned.1.call-update) | async-done | bytes 16400 | tf_op jit(solution)/shard_map/reduce_scatter | solution.py:21
  696.2 43.0 %all-gather.11 = f32[32,8,2]{1,2,0:T(2,128)S(1)} all-gather(f32[1,8,2]{1,2,0:T(2,128)S(1)} %bitcast.198), channel_id=7, replica_groups=mesh['site'=2,'wide'=32,'narrow'=4] {'wide'}, dimensions={0}, use_global_device_ids=true | all-gather | bytes 2112 | tf_op jit(solution)/shard_map/all_gather | solution.py:36
  743.9 51.4 %all_gather.71 = f32[8,8192]{1,0:T(8,128)} all-gather(f32[8,256]{1,0:T(8,128)S(1)} %fusion.14), channel_id=1, replica_groups=mesh['site'=2,'wide'=32,'narrow'=4] {'wide'}, dimensions={1}, use_global_device_ids=true | all-gather | bytes 270336 | tf_op jit(solution)/shard_map/all_gather | solution.py:40
  800.8 6.1 all-to-all-done.5
  (86 shorter events, 49.5 us)
Async XLA Ops:
  7.2 265.6 %copy-start = (f32[32,1,2048]{2,1,0:T(1,128)S(1)}, f32[32,1,2048]{2,1,0:T(1,128)}, u32[]{:S(2)}) copy-start(f32[32,1,2048]{2,1,0:T(1,128)} %param.3) | copy-start | bytes 786436
  7.2 31.8 %reduce-scatter.7.cloned.1.call-start = ((), (), s32[]{:S(2)}) async-start(), calls=%async_computation.18 | async-start | bytes 81920 | tf_op jit(solution)/shard_map/reduce_scatter | solution.py:21
  12.7 153.9 %reduce-scatter.9.cloned.1.call-start = ((), (), s32[]{:S(2)}) async-start(), calls=%async_computation.19 | async-start | bytes 81920 | tf_op jit(solution)/shard_map/reduce_scatter | solution.py:21
  262.7 10.1 %all-to-all-start.1 = ((f32[8,4,2048]{2,0,1:T(8,128)}), f32[8,4,2048]{2,0,1:T(8,128)S(1)}, u32[]{:S(2)}, u32[]{:S(2)}) async-start(f32[8,4,2048]{2,0,1:T(8,128)} %bitcast.21), calls=%async_computation.3 | async-start | bytes 524288 | tf_op jit(solution)/shard_map/all_to_all | solution.py:46
  266.1 34.8 %reduce-scatter.11.cloned.1.call-start = ((), (), s32[]{:S(2)}) async-start(), calls=%async_computation.20 | async-start | bytes 81920 | tf_op jit(solution)/shard_map/reduce_scatter | solution.py:21
  272.9 1.6 collective-permute-start
  279.8 148.7 %reduce-scatter.13.cloned.1.call-start = ((), (), s32[]{:S(2)}) async-start(), calls=%async_computation.21 | async-start | bytes 81920 | tf_op jit(solution)/shard_map/reduce_scatter | solution.py:21
  407.5 150.2 %reduce-scatter.15.cloned.1.call-start = ((), (), s32[]{:S(2)}) async-start(), calls=%async_computation.22 | async-start | bytes 81920 | tf_op jit(solution)/shard_map/reduce_scatter | solution.py:21
  529.8 1.5 collective-permute-start.1
  544.9 8.4 %all-to-all-start.7 = ((f32[8,4,1]{0,2,1:T(1,128)}), f32[8,4,1]{0,2,1:T(1,128)S(1)}, u32[]{:S(2)}, u32[]{:S(2)}) async-start(f32[8,4,1]{0,2,1:T(1,128)} %broadcast_in_dim.97), calls=%async_computation.13 | async-start | bytes 4096 | tf_op jit(solution)/shard_map/all_to_all | solution.py:47
  553.4 120.9 %collective-permute-start.2 = (f32[32]{0:T(128)S(1)}, f32[32]{0:T(128)S(1)}, u32[]{:S(2)}, u32[]{:S(2)}) collective-permute-start(f32[32]{0:T(128)S(1)} %select_n.125), channel_id=1, source_target_pairs={{0,128},{128,0},{1,129},{129,1},{2,130},{130,2},{3,131},{131,3},{4... | collective-permute-start | bytes 392 | tf_op jit(solution)/shard_map/ppermute | solution.py:14
  554.0 48.3 %all-to-all-start.8 = ((f32[8,4,1]{0,2,1:T(1,128)}), f32[8,4,1]{0,2,1:T(1,128)S(1)}, u32[]{:S(2)}, u32[]{:S(2)}) async-start(f32[8,4,1]{0,2,1:T(1,128)} %broadcast_in_dim.99), calls=%async_computation.14 | async-start | bytes 4096 | tf_op jit(solution)/shard_map/all_to_all | solution.py:47
  602.9 54.7 %all-to-all-start.9 = ((f32[8,4,1]{0,2,1:T(1,128)}), f32[8,4,1]{0,2,1:T(1,128)S(1)}, u32[]{:S(2)}, u32[]{:S(2)}) async-start(f32[8,4,1]{0,2,1:T(1,128)} %broadcast_in_dim.100), calls=%async_computation.15 | async-start | bytes 4096 | tf_op jit(solution)/shard_map/all_to_all | solution.py:47
  657.6 11.4 %all-to-all-start.4 = ((f32[8,4,2048]{2,0,1:T(8,128)}), f32[8,4,2048]{2,0,1:T(8,128)S(1)}, u32[]{:S(2)}, u32[]{:S(2)}) async-start(f32[8,4,2048]{2,0,1:T(8,128)} %bitcast.50), calls=%async_computation.9 | async-start | bytes 524288 | tf_op jit(solution)/shard_map/all_to_all | solution.py:46
  662.4 33.1 %reduce-scatter.17.cloned.1.call-start = ((), (), s32[]{:S(2)}) async-start(), calls=%async_computation.23 | async-start | bytes 81920 | tf_op jit(solution)/shard_map/reduce_scatter | solution.py:21
  675.0 8.4 %all-to-all-start.10 = ((f32[8,4,1]{0,2,1:T(1,128)}), f32[8,4,1]{0,2,1:T(1,128)S(1)}, u32[]{:S(2)}, u32[]{:S(2)}) async-start(f32[8,4,1]{0,2,1:T(1,128)} %broadcast_in_dim.101), calls=%async_computation.16 | async-start | bytes 4096 | tf_op jit(solution)/shard_map/all_to_all | solution.py:47
  678.1 122.1 %collective-permute-start.3 = (f32[32]{0:T(128)S(1)}, f32[32]{0:T(128)S(1)}, u32[]{:S(2)}, u32[]{:S(2)}) collective-permute-start(f32[32]{0:T(128)S(1)} %add_add_fusion), channel_id=1, source_target_pairs={{0,128},{128,0},{1,129},{129,1},{2,130},{130,2},{3,131},{131,3},{4... | collective-permute-start | bytes 392 | tf_op jit(solution)/shard_map/ppermute | solution.py:14
  739.9 55.4 %all-to-all-start.11 = ((f32[8,4,1]{0,2,1:T(1,128)}), f32[8,4,1]{0,2,1:T(1,128)S(1)}, u32[]{:S(2)}, u32[]{:S(2)}) async-start(f32[8,4,1]{0,2,1:T(1,128)} %broadcast_in_dim.102), calls=%async_computation.17 | async-start | bytes 4096 | tf_op jit(solution)/shard_map/all_to_all | solution.py:47
  795.4 11.4 %all-to-all-start.5 = ((f32[8,4,2048]{2,0,1:T(8,128)}), f32[8,4,2048]{2,0,1:T(8,128)S(1)}, u32[]{:S(2)}, u32[]{:S(2)}) async-start(f32[8,4,2048]{2,0,1:T(8,128)} %bitcast.59), calls=%async_computation.11 | async-start | bytes 524288 | tf_op jit(solution)/shard_map/all_to_all | solution.py:46
Sparse Core Ops, SparseCore 0:
  12.8 26.1 reduce-scatter.6
  145.7 20.8 reduce-scatter.8
  279.9 20.9 reduce-scatter.10
  407.6 20.8 reduce-scatter.12
  536.8 20.8 reduce-scatter.14
  674.5 20.9 reduce-scatter.16
